TPU v7x, 32 devices: a whole 2x2x4 slice. The times are simulated.
32 devices in a mesh: dp: 4 (over y, core), feat: 8 (over z, x).
Axes of the slice: x: 2, y: 2, z: 4, core: 2. Of those that a mesh axis runs over, the one named last changes fastest.
Arguments:
- images: bfloat16 [1536, 3072], P('dp'), may hold values from -6 to 6
- labels: int32 [1536], P('dp'), may hold values from 0 to 9
- frequencies: bfloat16 [3072, 8192], P(None, 'feat'), may hold values from -0.15625 to 0.15625
- privacy_noise: float32 [10, 2, 8192], P(None, None, 'feat'), may hold values from -0.6 to 0.6
- latents: bfloat16 [1024, 256], P('dp'), may hold values from -6 to 6
- gen_labels: int32 [1024], P('dp'), may hold values from 0 to 9
- gen_in: bfloat16 [256, 1024], replicated, may hold values from -0.375 to 0.375
- gen_out: bfloat16 [1024, 3072], replicated, may hold values from -0.25 to 0.25
Outputs:
- match_loss: float32 [], replicated
- grad_in: float32 [256, 1024], P('dp')
- grad_out: float32 [1024, 3072], P('dp')
All inputs are finite; a program needn't handle non-finite values.
Results may differ from a plain program's by a relative error of at most 0.0035.
Values sent between devices are 32-bit elements; how exact they have to be, the bound alone decides.
No kernel may reach another device: no remote copies, remote signals or barrier semaphores. Data moves between devices by JAX's collectives and lax.ppermute only.
A program may use at most 128 MiB of HBM per device.

v0:
```python
import jax
import jax.numpy as jnp
from jax import lax
from jax.sharding import PartitionSpec as P


def class_sums(phase, classes_of, classes, scale):
    feats = jnp.concatenate([jnp.cos(phase), jnp.sin(phase)], axis=1)
    onehot = (classes_of[:, None] == jnp.arange(classes)[None, :]).astype(jnp.float32)
    sums = jnp.dot(onehot.T, feats, precision=lax.Precision.HIGHEST) * scale
    return (sums.reshape(classes, 2, phase.shape[1]), onehot)


def generator_grads(image_grad, image_out, hidden, pre_hidden, sigmoid_h, latents, gen_out):
    out_grad = (image_grad * (1.0 - image_out * image_out)).astype(jnp.bfloat16)
    grad_out = jnp.einsum("gh,gd->hd", hidden, out_grad, preferred_element_type=jnp.float32)
    back_hidden = jnp.einsum("gd,hd->gh", out_grad, gen_out, preferred_element_type=jnp.float32)
    hidden_grad = (back_hidden * sigmoid_h * (1.0 + pre_hidden * (1.0 - sigmoid_h))).astype(
        jnp.bfloat16
    )
    grad_in = jnp.einsum("gz,gh->zh", latents, hidden_grad, preferred_element_type=jnp.float32)
    return (grad_in, grad_out)


def per_device(images, labels, frequencies, privacy_noise, latents, gen_labels, gen_in, gen_out):
    classes = privacy_noise.shape[0]
    feat_dev = frequencies.shape[1]
    data_devices = lax.axis_size("dp")
    feat_devices = lax.axis_size("feat")
    total_images = images.shape[0] * data_devices
    total_gen = latents.shape[0] * data_devices
    total_feats = feat_dev * feat_devices
    data_phase = jnp.dot(images, frequencies, preferred_element_type=jnp.float32)
    data_part, unused = class_sums(data_phase, labels, classes, classes / total_images)
    pre_hidden = jnp.dot(latents, gen_in, preferred_element_type=jnp.float32)
    sigmoid_h = jax.nn.sigmoid(pre_hidden)
    hidden = (pre_hidden * sigmoid_h).astype(jnp.bfloat16)
    image_out = jnp.tanh(jnp.dot(hidden, gen_out, preferred_element_type=jnp.float32))
    gen_image = image_out.astype(jnp.bfloat16)
    gen_phase = jnp.dot(gen_image, frequencies, preferred_element_type=jnp.float32)
    gen_part, gen_onehot = class_sums(gen_phase, gen_labels, classes, classes / total_gen)
    mean_gap = lax.psum(gen_part - data_part, "dp") - privacy_noise
    match_loss = lax.psum(jnp.sum(mean_gap * mean_gap), "feat") / (2.0 * total_feats)
    gap_rows = jnp.dot(
        gen_onehot, mean_gap.reshape(classes, 2 * feat_dev), precision=lax.Precision.HIGHEST
    ) * (16.0 * classes / total_gen)
    phase_grad = (
        jnp.cos(gen_phase) * gap_rows[:, feat_dev:] - jnp.sin(gen_phase) * gap_rows[:, :feat_dev]
    ).astype(jnp.bfloat16)
    partial_image = jnp.einsum(
        "gf,df->gd", phase_grad, frequencies, preferred_element_type=jnp.float32
    )
    image_grad = lax.psum(partial_image, "feat")
    grad_in, grad_out = generator_grads(
        image_grad, image_out, hidden, pre_hidden, sigmoid_h, latents, gen_out
    )
    grad_in, grad_out = (
        lax.psum_scatter(grad_in, "dp", scatter_dimension=0, tiled=True),
        lax.psum_scatter(grad_out, "dp", scatter_dimension=0, tiled=True),
    )
    return (match_loss, grad_in, grad_out)


def solution(mesh):
    return jax.shard_map(
        per_device,
        mesh=mesh,
        in_specs=(
            P("dp", None),
            P("dp"),
            P(None, "feat"),
            P(None, None, "feat"),
            P("dp", None),
            P("dp"),
            P(),
            P(),
        ),
        out_specs=(P(), P("dp", None), P("dp", None)),
        check_vma=False,
    )
```

profile of v0, /device:TPU:0, one launch (start us, length us, event | category | flops | bytes accessed | tf_op | source)
XLA Modules:
  0.0 356.0 jit_solution(9388458838005756762)
XLA Ops:
  7.2 0.0 all-reduce.3.cloned.1.call-start
  7.2 1.6 fusion.34
  8.8 1.0 copy-done.4
  9.8 4.8 %convolution_tanh_fusion = f32[256,3072]{1,0:T(8,128)S(1)} fusion(bf16[1024,3072]{1,0:T(8,128)(2,1)} %param.15, f32[256,1024]{1,0:T(8,128)S(1)} %fusion.34), kind=kOutput, calls=%fused_computation | convolution fusion | flops 1611923456 | bytes 10485760 | tf_op jit(solution)/shard_map/dot_general | solution.py:38
  14.6 5.3 %fusion.33 = (f32[256,1024]{1,0:T(8,128)S(1)}, f32[256,1024]{1,0:T(8,128)S(1)}) fusion(bf16[3072,1024]{1,0:T(8,128)(2,1)S(1)} %bitcast.19, f32[256,3072]{1,0:T(8,128)S(1)} %convolution_tanh_fusion), kind=kOutput, calls=%fused_computation.41 | convolution fusion | flops 1611399168 | bytes 11534336 | tf_op jit(solution)/shard_map/dot_general | solution.py:40
  20.0 12.3 %fusion.32 = (f32[384,1024]{1,0:T(8,128)S(1)}, f32[384,1024]{1,0:T(8,128)S(1)}) fusion(bf16[384,3072]{1,0:T(8,128)(2,1)S(1)} %copy-done, bf16[3072,1024]{1,0:T(8,128)(2,1)S(1)} %bitcast.19), kind=kOutput, calls=%fused_computation.40 | convolution fusion | flops 2415919104 | bytes 11796480 | tf_op jit(solution)/shard_map/dot_general | solution.py:33
  32.3 0.8 convolution_multiply_fusion.1
  33.1 1.2 fusion.7
  34.3 0.7 sub.22
  35.0 0.2 all-reduce.5.cloned.1.call-start
  35.3 32.9 %all-reduce.3.cloned.1.call-done = f32[10,2,1024]{2,1,0:T(2,128)} async-done(((f32[10,2,1024]{2,1,0:T(2,128)}), f32[10,2,1024]{2,1,0:T(2,128)}) %all-reduce.3.cloned.1.call-update) | async-done | bytes 81936 | tf_op jit(solution)/shard_map/psum | solution.py:42
  68.2 1.7 multiply_reduce_fusion
  70.0 1.0 convolution_multiply_fusion
  71.0 6.4 %fusion.22 = f32[256,3072]{1,0:T(8,128)} fusion(bf16[3072,1024]{1,0:T(8,128)(2,1)} %param.10, f32[256,1024]{1,0:T(8,128)S(1)} %copy-done.3, f32[256,2048]{1,0:T(8,128)S(1)} %convolution_multiply_fusion, f32[256,1024]{1,0:T(8,128)S(1)} %get-tuple-element.13), kind=kOutput, calls=%fused_computation.28 | convolution fusion | flops 1611661312 | bytes 13631488 | tf_op jit(solution)/shard_map/gf,df->gd/dot_general | solution.py:50
  77.5 0.0 reduce-scatter.7.cloned.1.call-start
  77.5 130.2 %all-reduce.5.cloned.1.call-done = f32[256,3072]{1,0:T(8,128)} async-done(((f32[256,3072]{1,0:T(8,128)}), f32[256,3072]{1,0:T(8,128)}) %all-reduce.5.cloned.1.call-update) | async-done | bytes 3145744 | tf_op jit(solution)/shard_map/psum | solution.py:53
  207.7 4.6 %multiply_convert_fusion = bf16[256,3072]{1,0:T(8,128)(2,1)} fusion(f32[256,3072]{1,0:T(8,128)} %all-reduce.5.cloned.1.call-done, f32[256,3072]{1,0:T(8,128)} %copy-done.1), kind=kLoop, calls=%fused_computation.5 | loop fusion | flops 3145728 | bytes 7864320 | tf_op jit(solution)/shard_map/convert_element_type | solution.py:15
  212.3 6.6 %convolution_bitcast_fusion = f32[256,1024]{0,1:T(8,128)} fusion(bf16[256,256]{1,0:T(8,128)(2,1)S(1)} %copy-done.6, bf16[256,3072]{1,0:T(8,128)(2,1)} %multiply_convert_fusion, bf16[1024,3072]{1,0:T(8,128)(2,1)} %param.15, f32[256,1024]{1,0:T(8,128)S(1)} %copy-done.5), kind=kOutput, calls=%fused_computation.17 | convolution fusion | flops 1747189760 | bytes 10092544 | tf_op jit(solution)/shard_map/gz,gh->zh/dot_general | solution.py:21
  218.9 2.6 copy.13
  221.5 0.0 reduce-scatter.5.cloned.1.call-start
  221.5 8.0 %fusion.31 = f32[1024,3072]{1,0:T(8,128)} fusion(bf16[256,3072]{1,0:T(8,128)(2,1)} %multiply_convert_fusion, f32[256,1024]{1,0:T(8,128)S(1)} %copy-done.5), kind=kOutput, calls=%fused_computation.39 | convolution fusion | flops 1611923456 | bytes 15204352 | tf_op jit(solution)/shard_map/gh,gd->hd/dot_general | solution.py:16
  229.6 19.9 %psum.22 = f32[]{:T(128)} all-reduce(f32[]{:T(128)} %get-tuple-element.9), channel_id=1, replica_groups=mesh['dp'=4,'feat'=8] {'feat'}, use_global_device_ids=true, to_apply=%region_2.0 | all-reduce | flops 1 | bytes 8 | tf_op jit(solution)/shard_map/psum | solution.py:43
  250.1 0.0 reduce-scatter.7.cloned.1.call-done
  250.1 98.3 %reduce-scatter.5.cloned.1.call-done = f32[256,3072]{1,0:T(8,128)} async-done(((f32[1024,3072]{1,0:T(8,128)}), f32[256,3072]{1,0:T(8,128)}) %reduce-scatter.5.cloned.1.call-update) | async-done | bytes 3145744 | tf_op jit(solution)/shard_map/reduce_scatter | solution.py:59
  (28 shorter events, 0.2 us)
Async XLA Ops:
  7.2 12.8 %copy-start = (bf16[384,3072]{1,0:T(8,128)(2,1)S(1)}, bf16[384,3072]{1,0:T(8,128)(2,1)}, u32[]{:S(2)}) copy-start(bf16[384,3072]{1,0:T(8,128)(2,1)} %param.8) | copy-start | bytes 7077892
  7.2 61.0 %all-reduce.3.cloned.1.call-start = ((), (), s32[]{:S(2)}) async-start(), calls=%async_computation.2 | async-start | bytes 163840 | tf_op jit(solution)/shard_map/psum | solution.py:42
  7.2 7.4 %slice-start = ((s8[6291456]{0:T(1024)(128)(4,1)}), s8[4194304]{0:T(1024)(128)(4,1)S(1)}, s32[]{:S(2)}) async-start(s8[6291456]{0:T(1024)(128)(4,1)} %bitcast.18), calls=%async_computation.6 | async-start | bytes 8388608
  8.8 1.0 copy-start.4
  9.8 4.8 %slice-start.1 = ((s8[6291456]{0:T(1024)(128)(4,1)}), s8[2097152]{0:T(1024)(128)(4,1)S(1)}, s32[]{:S(2)}) async-start(s8[6291456]{0:T(1024)(128)(4,1)} %bitcast.18), calls=%async_computation.7 | async-start | bytes 4194304
  14.6 5.3 %copy-start.1 = (f32[256,3072]{1,0:T(8,128)}, f32[256,3072]{1,0:T(8,128)S(1)}, u32[]{:S(2)}) copy-start(f32[256,3072]{1,0:T(8,128)S(1)} %convolution_tanh_fusion) | copy-start | bytes 9437188
  20.0 12.3 %copy-start.2 = (f32[256,1024]{1,0:T(8,128)}, f32[256,1024]{1,0:T(8,128)S(1)}, u32[]{:S(2)}) copy-start(f32[256,1024]{1,0:T(8,128)S(1)} %get-tuple-element.14) | copy-start | bytes 3145732
  20.0 12.3 %copy-start.7 = (s32[256]{0:T(256)S(1)}, s32[256]{0:T(256)}, u32[]{:S(2)}) copy-start(s32[256]{0:T(256)} %param.13) | copy-start | bytes 3076
  20.0 13.2 %copy-start.8 = (s32[384]{0:T(512)S(1)}, s32[384]{0:T(512)}, u32[]{:S(2)}) copy-start(s32[384]{0:T(512)} %param.9) | copy-start | bytes 4612
  35.0 172.7 %all-reduce.5.cloned.1.call-start = ((), (), s32[]{:S(2)}) async-start(), calls=%async_computation.3 | async-start | bytes 6291456 | tf_op jit(solution)/shard_map/psum | solution.py:53
  68.2 2.8 copy-start.3
  77.5 134.8 %copy-start.5 = (f32[256,1024]{1,0:T(8,128)S(1)}, f32[256,1024]{1,0:T(8,128)}, u32[]{:S(2)}) copy-start(f32[256,1024]{1,0:T(8,128)} %copy-done.4) | copy-start | bytes 3145732
  77.5 134.8 %copy-start.6 = (bf16[256,256]{1,0:T(8,128)(2,1)S(1)}, bf16[256,256]{1,0:T(8,128)(2,1)}, u32[]{:S(2)}) copy-start(bf16[256,256]{1,0:T(8,128)(2,1)} %param.12) | copy-start | bytes 393220
  77.5 172.6 %reduce-scatter.7.cloned.1.call-start = ((), (), s32[]{:S(2)}) async-start(), calls=%async_computation.5 | async-start | bytes 1310720
  221.5 126.9 %reduce-scatter.5.cloned.1.call-start = ((), (), s32[]{:S(2)}) async-start(), calls=%async_computation.4 | async-start | bytes 15728640 | tf_op jit(solution)/shard_map/reduce_scatter | solution.py:59
Sparse Core Ops, SparseCore 0:
  35.2 32.9 all-reduce.2
  77.6 130.0 all-reduce.4
  221.6 23.8 reduce-scatter.6
  248.5 99.8 reduce-scatter.4
where the time goes:
time: 356 us
  waiting for transfers between devices  261 us (73%)
  matrix products  47.9 us (13%)
  blocking collectives  19.9 us (6%)
  between operations  15.7 us (4%)
  other arithmetic  6.29 us (2%)
  local copies, waits for them, and re-layouts  4.46 us (1%)
    psum x1, waiting for transfers between devices, per_device(): image_grad = lax.psum(partial_image, 'feat')  130 us
    reduce_scatter x1, waiting for transfers between devices, per_device(): lax.psum_scatter(grad_out, 'dp', scatter_dimension=0, tiled=True)  98.3 us
    psum x1, waiting for transfers between devices, per_device(): mean_gap = lax.psum(gen_part - data_part, 'dp') - privacy_noise  32.9 us
    psum x1, blocking collectives, per_device(): lax.psum(jnp.sum(mean_gap * mean_gap), 'feat') / (2.0 * total_feats)  19.9 us
    dot_general x1, matrix products, per_device(): jnp.dot(images, frequencies, preferred_element_type=jnp.float32)  12.3 us
    dot_general x1, matrix products, generator_grads(): jnp.einsum('gh,gd->hd', hidden, out_grad, preferred_element_type=jnp.floa...  8.02 us
  transfers between devices with their start and end apart: 4, of which 3 were waited for; matrix products, arithmetic and copies ran while one was open for 2% of the time, Pallas kernels for 0%

commit v1 on v0

--- a/solution.py
+++ b/solution.py
@@ -2,6 +2,7 @@
 import jax.numpy as jnp
 from jax import lax
 from jax.sharding import PartitionSpec as P
+from jax.lax import all_gather
 
 
 def class_sums(phase, classes_of, classes, scale):
@@ -50,7 +51,11 @@
     partial_image = jnp.einsum(
         "gf,df->gd", phase_grad, frequencies, preferred_element_type=jnp.float32
     )
-    image_grad = lax.psum(partial_image, "feat")
+
+    def update_object(xin, dev_axis):
+        return all_gather(xin, dev_axis).sum(axis=0)
+
+    image_grad = update_object(partial_image, "feat")
     grad_in, grad_out = generator_grads(
         image_grad, image_out, hidden, pre_hidden, sigmoid_h, latents, gen_out
     )

time: 356 us -> 719 us (2.02)
  waiting for transfers between devices: 261 us -> 614 us
  other arithmetic: 6.29 us -> 16.6 us
    all_gather x0 -> x1, waiting for transfers between devices: none -> 482 us  [update_object(): return all_gather(xin, dev_axis).sum(axis=0)]
    psum x1 -> x0, waiting for transfers between devices: 130 us -> none  [per_device(): image_grad = lax.psum(partial_image, 'feat')]
    reduce_sum x0 -> x1, other arithmetic: none -> 11.5 us  [update_object(): return all_gather(xin, dev_axis).sum(axis=0)]
  transfers between devices with their start and end apart: 4 -> 4, of which waited for: 3 -> 3; matrix products, arithmetic and copies ran while one was open for 2% -> 1% of each run, Pallas kernels for 0% -> 0%
where the time goes in v1:
time: 719 us; the launch traced here: 718 us
  waiting for transfers between devices  614 us (85%)
  matrix products  45.8 us (6%)
  blocking collectives  20.8 us (3%)
  other arithmetic  16.6 us (2%)
  between operations  15.8 us (2%)
    all_gather x1, waiting for transfers between devices, update_object(): return all_gather(xin, dev_axis).sum(axis=0)  482 us
    reduce_scatter x1, waiting for transfers between devices, per_device(): lax.psum_scatter(grad_out, 'dp', scatter_dimension=0, tiled=True)  99.5 us
    psum x1, waiting for transfers between devices, per_device(): mean_gap = lax.psum(gen_part - data_part, 'dp') - privacy_noise  32.9 us
    psum x1, blocking collectives, per_device(): lax.psum(jnp.sum(mean_gap * mean_gap), 'feat') / (2.0 * total_feats)  20.8 us
  transfers between devices with their start and end apart: 4, of which 3 were waited for; matrix products, arithmetic and copies ran while one was open for 1% of the time, Pallas kernels for 0%

profile of v1, /device:TPU:0, one launch (start us, length us, event | category | flops | bytes accessed | tf_op | source)
XLA Modules:
  0.0 718.2 jit_solution(788916686689775193)
XLA Ops:
  7.2 0.0 all-reduce.2.cloned.1.call-start
  7.2 1.6 fusion.34
  8.8 1.0 copy-done.5
  9.8 4.8 convolution_tanh_fusion
  14.6 5.3 fusion.33
  20.0 12.3 %fusion.32 = (f32[384,1024]{1,0:T(8,128)S(1)}, f32[384,1024]{1,0:T(8,128)S(1)}) fusion(bf16[384,3072]{1,0:T(8,128)(2,1)S(1)} %copy-done, bf16[3072,1024]{1,0:T(8,128)(2,1)S(1)} %bitcast.20), kind=kOutput, calls=%fused_computation.40 | convolution fusion | flops 2415919104 | bytes 11796480 | tf_op jit(solution)/shard_map/dot_general | solution.py:34
  32.3 0.8 convolution_multiply_fusion.1
  33.2 1.2 fusion.7
  34.3 0.7 sub.22
  35.1 0.2 all-gather.3.cloned.1.call-start
  35.3 32.9 %all-reduce.2.cloned.1.call-done = f32[10,2,1024]{2,1,0:T(2,128)} async-done(((f32[10,2,1024]{2,1,0:T(2,128)}), f32[10,2,1024]{2,1,0:T(2,128)}) %all-reduce.2.cloned.1.call-update) | async-done | bytes 81936 | tf_op jit(solution)/shard_map/psum | solution.py:43
  68.2 1.6 multiply_reduce_fusion
  69.9 1.0 convolution_multiply_fusion
  70.9 6.4 fusion.22
  77.4 0.0 reduce-scatter.7.cloned.1.call-start
  77.4 481.8 %all-gather.3.cloned.1.call-done = f32[2048,3072]{1,0:T(8,128)} async-done(((f32[256,3072]{1,0:T(8,128)}), f32[2048,3072]{1,0:T(8,128)}) %all-gather.3.cloned.1.call-update) | async-done | bytes 25165840 | tf_op jit(solution)/shard_map/all_gather | solution.py:56
  559.2 11.5 %reduce_sum.19 = f32[256,3072]{1,0:T(8,128)} reduce(f32[8,256,3072]{2,1,0:T(8,128)} %bitcast.21, f32[]{:T(128)} %constant.3.clone.1), dimensions={0}, to_apply=%region_3.0 | reduce | flops 5505024 | bytes 28311556 | tf_op jit(solution)/shard_map/reduce_sum | solution.py:56
  570.7 3.5 multiply_convert_fusion
  574.3 6.1 convolution_bitcast_fusion
  580.3 2.6 copy.13
  583.0 0.0 reduce-scatter.5.cloned.1.call-start
  583.0 6.4 fusion.31
  589.5 20.8 %psum.15 = f32[]{:T(128)} all-reduce(f32[]{:T(128)} %get-tuple-element.9), channel_id=1, replica_groups=mesh['dp'=4,'feat'=8] {'feat'}, use_global_device_ids=true, to_apply=%region_2.0 | all-reduce | flops 1 | bytes 8 | tf_op jit(solution)/shard_map/psum | solution.py:44
  611.0 99.5 %reduce-scatter.5.cloned.1.call-done = f32[256,3072]{1,0:T(8,128)} async-done(((f32[1024,3072]{1,0:T(8,128)}), f32[256,3072]{1,0:T(8,128)}) %reduce-scatter.5.cloned.1.call-update) | async-done | bytes 3145744 | tf_op jit(solution)/shard_map/reduce_scatter | solution.py:64
  (33 shorter events, 0.2 us)
Async XLA Ops:
  7.2 12.8 %copy-start = (bf16[384,3072]{1,0:T(8,128)(2,1)S(1)}, bf16[384,3072]{1,0:T(8,128)(2,1)}, u32[]{:S(2)}) copy-start(bf16[384,3072]{1,0:T(8,128)(2,1)} %param.8) | copy-start | bytes 7077892
  7.2 61.0 %all-reduce.2.cloned.1.call-start = ((), (), s32[]{:S(2)}) async-start(), calls=%async_computation.2 | async-start | bytes 163840 | tf_op jit(solution)/shard_map/psum | solution.py:43
  7.2 7.4 %slice-start = ((s8[6291456]{0:T(1024)(128)(4,1)}), s8[4194304]{0:T(1024)(128)(4,1)S(1)}, s32[]{:S(2)}) async-start(s8[6291456]{0:T(1024)(128)(4,1)} %bitcast.19), calls=%async_computation.6 | async-start | bytes 8388608
  8.8 1.0 copy-start.5
  9.8 4.8 slice-start.1
  14.6 5.3 copy-start.2
  19.9 12.3 %copy-start.3 = (f32[256,1024]{1,0:T(8,128)}, f32[256,1024]{1,0:T(8,128)S(1)}, u32[]{:S(2)}) copy-start(f32[256,1024]{1,0:T(8,128)S(1)} %get-tuple-element.14) | copy-start | bytes 3145732
  20.0 12.3 %copy-start.9 = (s32[256]{0:T(256)S(1)}, s32[256]{0:T(256)}, u32[]{:S(2)}) copy-start(s32[256]{0:T(256)} %param.13) | copy-start | bytes 3076
  20.0 13.2 %copy-start.10 = (s32[384]{0:T(512)S(1)}, s32[384]{0:T(512)}, u32[]{:S(2)}) copy-start(s32[384]{0:T(512)} %param.9) | copy-start | bytes 4612
  32.3 35.9 %copy-start.8 = (f32[10,2,1024]{2,1,0:T(2,128)S(1)}, f32[10,2,1024]{2,1,0:T(2,128)}, u32[]{:S(2)}) copy-start(f32[10,2,1024]{2,1,0:T(2,128)} %param.11) | copy-start | bytes 245764
  33.1 37.8 %copy-start.4 = (f32[256,1024]{1,0:T(8,128)S(1)}, f32[256,1024]{1,0:T(8,128)}, u32[]{:S(2)}) copy-start(f32[256,1024]{1,0:T(8,128)} %copy-done.3) | copy-start | bytes 3145732
  35.1 524.2 %all-gather.3.cloned.1.call-start = ((), (), s32[]{:S(2)}) async-start(), calls=%async_computation.4 | async-start | bytes 28311552 | tf_op jit(solution)/shard_map/all_gather | solution.py:56
  77.4 533.6 %reduce-scatter.7.cloned.1.call-start = ((), (), s32[]{:S(2)}) async-start(), calls=%async_computation.5 | async-start | bytes 1310720
  570.7 3.5 copy-start.6
  570.7 3.5 copy-start.7
  583.0 127.6 %reduce-scatter.5.cloned.1.call-start = ((), (), s32[]{:S(2)}) async-start(), calls=%async_computation.3 | async-start | bytes 15728640 | tf_op jit(solution)/shard_map/reduce_scatter | solution.py:64
  589.5 121.1 %copy-start.1 = (bf16[384,3072]{1,0:T(8,128)(2,1)S(1)}, bf16[384,3072]{1,0:T(8,128)(2,1)}, u32[]{:S(2)}) copy-start(bf16[384,3072]{1,0:T(8,128)(2,1)} %param.8) | copy-start | bytes 7077892
Sparse Core Ops, SparseCore 0:
  35.2 32.9 all-reduce.1
  77.5 481.7 all-gather.2
  583.1 24.7 reduce-scatter.6
  610.9 99.6 reduce-scatter.4
